TPU v7x, 32 devices: a whole 2x2x4 slice. The times are simulated.
32 devices in a mesh: fsdp: 2 (over y), ctx: 4 (over z), tp: 4 (over x, core).
Axes of the slice: x: 2, y: 2, z: 4, core: 2. Of those that a mesh axis runs over, the one named last changes fastest.
Arguments:
- tokens: bfloat16 [4, 4, 1024, 1024], P(None, 'fsdp', 'ctx', 'tp'), may hold values from -6 to 6
- skip_tokens: bfloat16 [4, 4, 1024, 1024], P(None, 'fsdp', 'ctx', 'tp'), may hold values from -6 to 6
- merger_weight: bfloat16 [1024, 2, 1024], P(('fsdp', 'ctx'), None, 'tp'), may hold values from -0.125 to 0.125
- merger_bias: float32 [1024], P(('fsdp', 'ctx', 'tp')), may hold values from -3 to 3
- first_gain: float32 [1024], P(('fsdp', 'ctx', 'tp')), may hold values from 0.25 to 1.75
- first_shift: float32 [1024], P(('fsdp', 'ctx', 'tp')), may hold values from -2 to 2
- attend_weight: bfloat16 [1024, 3, 1024], P(('fsdp', 'ctx'), None, 'tp'), may hold values from -0.25 to 0.25
- output_weight: bfloat16 [1024, 1024], P(('fsdp', 'ctx'), 'tp'), may hold values from -0.75 to 0.75
- output_bias: float32 [1024], P(('fsdp', 'ctx', 'tp')), may hold values from -2 to 2
- second_gain: float32 [1024], P(('fsdp', 'ctx', 'tp')), may hold values from 0.25 to 1.75
- second_shift: float32 [1024], P(('fsdp', 'ctx', 'tp')), may hold values from -2 to 2
- expand_weight: bfloat16 [1024, 4096], P(('fsdp', 'ctx'), 'tp'), may hold values from -0.1875 to 0.1875
- widen_bias: float32 [4096], P(('fsdp', 'ctx', 'tp')), may hold values from -3 to 3
- shrink_weight: bfloat16 [1024, 4096], P(('fsdp', 'ctx'), 'tp'), may hold values from -0.125 to 0.125
- shrink_bias: float32 [1024], P(('fsdp', 'ctx', 'tp')), may hold values from -2 to 2
- live_slots: int32 [4, 4], P(None, 'fsdp'), may hold values from 0 to 1, as said below
- cotangent: bfloat16 [4, 4, 1024, 1024], P(None, 'fsdp', ('ctx', 'tp')), may hold values from -6 to 6
Outputs:
- layer_out: bfloat16 [4, 4, 1024, 1024], P(None, 'fsdp', ('ctx', 'tp'))
- grad_tokens: float32 [4, 4, 1024, 1024], P(None, 'fsdp', 'ctx', 'tp')
- grad_skip: float32 [4, 4, 1024, 1024], P(None, 'fsdp', 'ctx', 'tp')
- weight_merger: float32 [1024, 2, 1024], P(('fsdp', 'ctx'), None, 'tp')
- bias_merger: float32 [1024], P(('fsdp', 'ctx', 'tp'))
- gain_first: float32 [1024], P(('fsdp', 'ctx', 'tp'))
- shift_first: float32 [1024], P(('fsdp', 'ctx', 'tp'))
- weight_attend: float32 [1024, 3, 1024], P(('fsdp', 'ctx'), None, 'tp')
- weight_output: float32 [1024, 1024], P(('fsdp', 'ctx'), 'tp')
- bias_output: float32 [1024], P(('fsdp', 'ctx', 'tp'))
- gain_second: float32 [1024], P(('fsdp', 'ctx', 'tp'))
- shift_second: float32 [1024], P(('fsdp', 'ctx', 'tp'))
- weight_expand: float32 [1024, 4096], P(('fsdp', 'ctx'), 'tp')
- bias_expand: float32 [4096], P(('fsdp', 'ctx', 'tp'))
- weight_shrink: float32 [1024, 4096], P(('fsdp', 'ctx'), 'tp')
- bias_shrink: float32 [1024], P(('fsdp', 'ctx', 'tp'))
Inputs may be any that keep to these rules, and one draw needn't show every extreme that they name: `live_slots`: in every micro-batch but the last exactly one of the 4 slots is empty (0), in the last exactly two; the empty slots lie anywhere.
All inputs are finite; a program needn't handle non-finite values.
Results may differ from a plain program's by a relative error of at most 0.017.
Values may be sent and summed in bfloat16 or wider, within the bound.
No kernel may reach another device: no remote copies, remote signals or barrier semaphores. Data moves between devices by JAX's collectives and lax.ppermute only.
A program may use at most 256 MiB of HBM per device.

v0:
```python
import jax
import jax.numpy as jnp
from jax import lax
from jax.sharding import PartitionSpec as P

HD = 64
EPSILON = 1e-05


def layer_norm(matrix, scales, shifts):
    center = matrix - jnp.mean(matrix, axis=-1, keepdims=True)
    spread = jnp.mean(center * center, axis=-1, keepdims=True)
    return center * lax.rsqrt(spread + EPSILON) * scales + shifts


def gelu_exact(matrix):
    return jax.nn.gelu(matrix, approximate=False)


def fetch(merger_part, attend_part, output_part, expand_part, shrink_part):
    return (
        lax.all_gather(merger_part, ("fsdp", "ctx"), axis=0, tiled=True),
        lax.all_gather(attend_part, ("fsdp", "ctx"), axis=0, tiled=True),
        lax.all_gather(output_part, ("fsdp", "ctx"), axis=0, tiled=True),
        lax.all_gather(expand_part, ("fsdp", "ctx"), axis=0, tiled=True),
        lax.all_gather(shrink_part, ("fsdp", "ctx"), axis=0, tiled=True),
    )


def spread_rows(block):
    return lax.all_gather(block, "tp", axis=1, tiled=True)


def fold_rows(block):
    return lax.psum_scatter(block, "tp", scatter_dimension=1, tiled=True)


def reduce_weights(parts):
    return (
        lax.psum_scatter(parts[0], ("fsdp", "ctx"), scatter_dimension=0, tiled=True),
        lax.psum_scatter(parts[1], ("fsdp", "ctx"), scatter_dimension=0, tiled=True),
        lax.psum_scatter(parts[2], ("fsdp", "ctx"), scatter_dimension=0, tiled=True),
        lax.psum_scatter(parts[3], ("fsdp", "ctx"), scatter_dimension=0, tiled=True),
        lax.psum_scatter(parts[4], ("fsdp", "ctx"), scatter_dimension=0, tiled=True),
    )


def micro_step(weights, vectors, tokens_now, skips_now, live_now, cot_now, tensor_rank):
    merger_full, attend_full, output_full, expand_full, shrink_full = weights
    (
        merger_bias,
        first_gain,
        first_shift,
        output_bias,
        second_gain,
        second_shift,
        shrink_bias,
        widen_bias,
    ) = vectors
    groups = tokens_now.shape[0]
    local_len = tokens_now.shape[1]
    heads_dev = attend_full.shape[2] // HD
    hidden = expand_full.shape[1]
    scaling = HD ** (-0.5)
    stacked = jnp.stack([tokens_now, skips_now], axis=2)
    joined = (
        fold_rows(
            jnp.einsum("stci,oci->sto", stacked, merger_full, preferred_element_type=jnp.float32)
        )
        + merger_bias
    )
    normed, first_pull = jax.vjp(layer_norm, joined, first_gain, first_shift)
    normed_all = spread_rows(normed.astype(jnp.bfloat16))
    project = jnp.einsum(
        "std,dcj->stcj", normed_all, attend_full, preferred_element_type=jnp.float32
    ).astype(jnp.bfloat16)
    key_rows, value_rows = (
        lax.all_gather(project[:, :, 1], "ctx", axis=1, tiled=True),
        lax.all_gather(project[:, :, 2], "ctx", axis=1, tiled=True),
    )
    seq_len = key_rows.shape[1]
    query_heads = project[:, :, 0].reshape(groups, local_len, heads_dev, HD)
    key_heads = key_rows.reshape(groups, seq_len, heads_dev, HD)
    value_heads = value_rows.reshape(groups, seq_len, heads_dev, HD)
    scores = (
        jnp.einsum("sqhd,skhd->shqk", query_heads, key_heads, preferred_element_type=jnp.float32)
        * scaling
    )
    row_peak = jnp.max(scores, axis=-1, keepdims=True)
    logsum = row_peak + jnp.log(jnp.sum(jnp.exp(scores - row_peak), axis=-1, keepdims=True))
    probs_low = jnp.exp(scores - logsum).astype(jnp.bfloat16)
    attended = jnp.einsum(
        "shqk,skhd->sqhd", probs_low, value_heads, preferred_element_type=jnp.float32
    )
    attended = attended.astype(jnp.bfloat16).reshape(groups, local_len, heads_dev * HD)
    second = (
        joined
        + fold_rows(
            jnp.einsum("sti,oi->sto", attended, output_full, preferred_element_type=jnp.float32)
        )
        + output_bias
    )
    normed_two, second_pull = jax.vjp(layer_norm, second, second_gain, second_shift)
    normed_two_all = spread_rows(normed_two.astype(jnp.bfloat16))
    bias_slice = lax.dynamic_slice_in_dim(widen_bias, tensor_rank * hidden, hidden)
    widened_hidden = (
        jnp.einsum("std,df->stf", normed_two_all, expand_full, preferred_element_type=jnp.float32)
        + bias_slice
    )
    activated, gelu_pull = jax.vjp(gelu_exact, widened_hidden)
    activated_low = activated.astype(jnp.bfloat16)
    result = (
        second
        + fold_rows(
            jnp.einsum(
                "stf,of->sto", activated_low, shrink_full, preferred_element_type=jnp.float32
            )
        )
        + shrink_bias
    )
    live_mask = live_now.astype(jnp.float32)[:, None, None]
    layer_out = (result * live_mask).astype(jnp.bfloat16)
    upstream = cot_now.astype(jnp.float32) * live_mask
    grad_shrink_bias = jnp.sum(upstream, axis=(0, 1))
    branch_low = spread_rows(upstream.astype(jnp.bfloat16))
    grad_shrink = jnp.einsum(
        "sto,stf->of", branch_low, activated_low, preferred_element_type=jnp.float32
    )
    grad_activated = jnp.einsum(
        "sto,of->stf", branch_low, shrink_full, preferred_element_type=jnp.float32
    )
    grad_expanded = gelu_pull(grad_activated)[0].astype(jnp.bfloat16)
    grad_expand_bias = jnp.sum(grad_expanded, axis=(0, 1), dtype=jnp.float32)
    grad_expand = jnp.einsum(
        "std,stf->df", normed_two_all, grad_expanded, preferred_element_type=jnp.float32
    )
    grad_normed_two = fold_rows(
        jnp.einsum("stf,df->std", grad_expanded, expand_full, preferred_element_type=jnp.float32)
    )
    grad_second_norm, grad_second_gain, grad_second_shift = second_pull(grad_normed_two)
    grad_second = upstream + grad_second_norm
    grad_output_bias = jnp.sum(grad_second, axis=(0, 1))
    attn_low = spread_rows(grad_second.astype(jnp.bfloat16))
    grad_output = jnp.einsum("sto,sti->oi", attn_low, attended, preferred_element_type=jnp.float32)
    grad_attended = jnp.einsum(
        "sto,oi->sti", attn_low, output_full, preferred_element_type=jnp.float32
    )
    grad_attended = grad_attended.astype(jnp.bfloat16).reshape(groups, local_len, heads_dev, HD)
    scores_again = (
        jnp.einsum("sqhd,skhd->shqk", query_heads, key_heads, preferred_element_type=jnp.float32)
        * scaling
    )
    probs = jnp.exp(scores_again - logsum)
    grad_probs = jnp.einsum(
        "sqhd,skhd->shqk", grad_attended, value_heads, preferred_element_type=jnp.float32
    )
    row_inner = jnp.sum(probs * grad_probs, axis=-1, keepdims=True)
    grad_scores = (probs * (grad_probs - row_inner)).astype(jnp.bfloat16)
    grad_queries = (
        jnp.einsum("shqk,skhd->sqhd", grad_scores, key_heads, preferred_element_type=jnp.float32)
        * scaling
    )
    probs_again = probs.astype(jnp.bfloat16)
    key_terms = (
        jnp.einsum("shqk,sqhd->skhd", grad_scores, query_heads, preferred_element_type=jnp.float32)
        * scaling
    )
    value_terms = jnp.einsum(
        "shqk,sqhd->skhd", probs_again, grad_attended, preferred_element_type=jnp.float32
    )
    grad_keys, grad_values = (
        lax.psum_scatter(
            key_terms.reshape(groups, seq_len, heads_dev * HD).astype(jnp.bfloat16),
            "ctx",
            scatter_dimension=1,
            tiled=True,
        ).astype(jnp.float32),
        lax.psum_scatter(
            value_terms.reshape(groups, seq_len, heads_dev * HD).astype(jnp.bfloat16),
            "ctx",
            scatter_dimension=1,
            tiled=True,
        ).astype(jnp.float32),
    )
    grad_project = jnp.stack(
        [
            grad_queries.reshape(groups, local_len, heads_dev * HD).astype(jnp.bfloat16),
            grad_keys.astype(jnp.bfloat16),
            grad_values.astype(jnp.bfloat16),
        ],
        axis=2,
    )
    grad_attend = jnp.einsum(
        "std,stcj->dcj", normed_all, grad_project, preferred_element_type=jnp.float32
    )
    grad_normed = fold_rows(
        jnp.einsum("stcj,dcj->std", grad_project, attend_full, preferred_element_type=jnp.float32)
    )
    grad_first_norm, gradient_leading_gain, grad_first_shift = first_pull(grad_normed)
    grad_joined = grad_second + grad_first_norm
    grad_merger_bias = jnp.sum(grad_joined, axis=(0, 1))
    joined_low = spread_rows(grad_joined.astype(jnp.bfloat16))
    grad_merger = jnp.einsum(
        "sto,stci->oci", joined_low, stacked, preferred_element_type=jnp.float32
    )
    grad_stacked = jnp.einsum(
        "sto,oci->stci", joined_low, merger_full, preferred_element_type=jnp.float32
    )
    expand_whole = lax.dynamic_update_slice_in_dim(
        jnp.zeros((widen_bias.shape[0],), jnp.float32), grad_expand_bias, tensor_rank * hidden, 0
    )
    weight_part = (grad_merger, grad_attend, grad_output, grad_expand, grad_shrink)
    vector_portion = (
        grad_merger_bias,
        gradient_leading_gain,
        grad_first_shift,
        grad_output_bias,
        grad_second_gain,
        grad_second_shift,
        grad_shrink_bias,
        expand_whole,
    )
    return (layer_out, grad_stacked[:, :, 0], grad_stacked[:, :, 1], weight_part, vector_portion)


def on_device(
    tokens,
    skip_tokens,
    merger_weight,
    merger_bias,
    first_gain,
    first_shift,
    attend_weight,
    output_weight,
    output_bias,
    second_gain,
    second_shift,
    expand_weight,
    widen_bias,
    shrink_weight,
    shrink_bias,
    live_slots,
    cotangent,
):
    tensor_rank = lax.axis_index("tp")
    vectors = (
        lax.all_gather(merger_bias, ("fsdp", "ctx", "tp"), axis=0, tiled=True),
        lax.all_gather(first_gain, ("fsdp", "ctx", "tp"), axis=0, tiled=True),
        lax.all_gather(first_shift, ("fsdp", "ctx", "tp"), axis=0, tiled=True),
        lax.all_gather(output_bias, ("fsdp", "ctx", "tp"), axis=0, tiled=True),
        lax.all_gather(second_gain, ("fsdp", "ctx", "tp"), axis=0, tiled=True),
        lax.all_gather(second_shift, ("fsdp", "ctx", "tp"), axis=0, tiled=True),
        lax.all_gather(shrink_bias, ("fsdp", "ctx", "tp"), axis=0, tiled=True),
        lax.all_gather(widen_bias, ("fsdp", "ctx", "tp"), axis=0, tiled=True),
    )
    batches = tokens.shape[0]
    outs_list = []
    token_list = []
    skip_list = []
    weight_totals = None
    vector_totals = None
    for batch_index in range(batches):
        current = fetch(merger_weight, attend_weight, output_weight, expand_weight, shrink_weight)
        layer_out, grad_one, gradient_remaining, weight_part, vector_portion = micro_step(
            current,
            vectors,
            tokens[batch_index],
            skip_tokens[batch_index],
            live_slots[batch_index],
            cotangent[batch_index],
            tensor_rank,
        )
        if weight_totals is None:
            weight_totals = weight_part
            vector_totals = vector_portion
        else:
            weight_totals = tuple(
                (former + latter for former, latter in zip(weight_totals, weight_part))
            )
            vector_totals = tuple(
                (former + latter for former, latter in zip(vector_totals, vector_portion))
            )
        outs_list.append(layer_out)
        token_list.append(grad_one)
        skip_list.append(gradient_remaining)
    weight_totals = reduce_weights(weight_totals)
    vector_grads = (
        lax.psum_scatter(vector_totals[0], ("fsdp", "ctx", "tp"), scatter_dimension=0, tiled=True),
        lax.psum_scatter(vector_totals[1], ("fsdp", "ctx", "tp"), scatter_dimension=0, tiled=True),
        lax.psum_scatter(vector_totals[2], ("fsdp", "ctx", "tp"), scatter_dimension=0, tiled=True),
        lax.psum_scatter(vector_totals[3], ("fsdp", "ctx", "tp"), scatter_dimension=0, tiled=True),
        lax.psum_scatter(vector_totals[4], ("fsdp", "ctx", "tp"), scatter_dimension=0, tiled=True),
        lax.psum_scatter(vector_totals[5], ("fsdp", "ctx", "tp"), scatter_dimension=0, tiled=True),
        lax.psum_scatter(vector_totals[6], ("fsdp", "ctx", "tp"), scatter_dimension=0, tiled=True),
        lax.psum_scatter(vector_totals[7], ("fsdp", "ctx", "tp"), scatter_dimension=0, tiled=True),
    )
    return (
        jnp.stack(outs_list, axis=0),
        jnp.stack(token_list, axis=0),
        jnp.stack(skip_list, axis=0),
        weight_totals[0],
        vector_grads[0],
        vector_grads[1],
        vector_grads[2],
        weight_totals[1],
        weight_totals[2],
        vector_grads[3],
        vector_grads[4],
        vector_grads[5],
        weight_totals[3],
        vector_grads[7],
        weight_totals[4],
        vector_grads[6],
    )


def solution(mesh):
    placed = (
        P(None, "fsdp", "ctx", "tp"),
        P(None, "fsdp", "ctx", "tp"),
        P(("fsdp", "ctx"), None, "tp"),
        P(("fsdp", "ctx", "tp")),
        P(("fsdp", "ctx", "tp")),
        P(("fsdp", "ctx", "tp")),
        P(("fsdp", "ctx"), None, "tp"),
        P(("fsdp", "ctx"), "tp"),
        P(("fsdp", "ctx", "tp")),
        P(("fsdp", "ctx", "tp")),
        P(("fsdp", "ctx", "tp")),
        P(("fsdp", "ctx"), "tp"),
        P(("fsdp", "ctx", "tp")),
        P(("fsdp", "ctx"), "tp"),
        P(("fsdp", "ctx", "tp")),
        P(None, "fsdp"),
        P(None, "fsdp", ("ctx", "tp"), None),
    )
    return jax.shard_map(
        on_device,
        mesh=mesh,
        in_specs=placed,
        out_specs=(
            P(None, "fsdp", ("ctx", "tp"), None),
            P(None, "fsdp", "ctx", "tp"),
            P(None, "fsdp", "ctx", "tp"),
            P(("fsdp", "ctx"), None, "tp"),
            P(("fsdp", "ctx", "tp")),
            P(("fsdp", "ctx", "tp")),
            P(("fsdp", "ctx", "tp")),
            P(("fsdp", "ctx"), None, "tp"),
            P(("fsdp", "ctx"), "tp"),
            P(("fsdp", "ctx", "tp")),
            P(("fsdp", "ctx", "tp")),
            P(("fsdp", "ctx", "tp")),
            P(("fsdp", "ctx"), "tp"),
            P(("fsdp", "ctx", "tp")),
            P(("fsdp", "ctx"), "tp"),
            P(("fsdp", "ctx", "tp")),
        ),
        check_vma=False,
    )
```

profile of v0, /device:TPU:0, one launch (start us, length us, event | category | flops | bytes accessed | tf_op | source)
XLA Modules:
  0.0 2147.7 jit_solution(7706245499468301437)
XLA Ops:
  10.6 43.0 %all-gather.42.cloned.1.call-done = bf16[1024,2,256]{2,0,1:T(8,128)(2,1)} async-done(((bf16[128,2,256]{2,0,1:T(8,128)(2,1)}), bf16[1024,2,256]{2,0,1:T(8,128)(2,1)}) %all-gather.42.cloned.1.call-update) | async-done | bytes 1048592 | tf_op jit(solution)/shard_map/all_gather | solution.py:22
  66.0 38.9 %all-reduce.16 = (f32[1024]{0:T(1024)S(1)}, f32[1024]{0:T(1024)S(1)}, f32[1024]{0:T(1024)S(1)}, f32[1024]{0:T(1024)S(1)}, f32[1024]{0:T(1024)S(1)}, /*index=5*/f32[1024]{0:T(1024)S(1)}) all-reduce(f32[1024]{0:T(1024)S(1)} %dynamic-update-slice.3, ...), channel_id=1, replica_groups=mesh['fsdp'=2,'ctx'=4,'tp'=4] {'fsdp','ctx','tp'}, use_global_device_ids=true, to_apply=%add | all-reduce | flops 6144 | bytes 49152
  122.3 33.8 %reduce-scatter.46.cloned.1.call-done = f32[2,64,1024]{2,1,0:T(8,128)} async-done(((f32[2,256,1024]{2,1,0:T(8,128)}), f32[2,64,1024]{2,1,0:T(8,128)}) %reduce-scatter.46.cloned.1.call-update) | async-done | bytes 524304 | tf_op jit(solution)/shard_map/reduce_scatter | solution.py:35
  156.1 34.0 %reduce-scatter.52.cloned.1.call-done = f32[2,64,1024]{2,1,0:T(8,128)} async-done(((f32[2,256,1024]{2,1,0:T(8,128)}), f32[2,64,1024]{2,1,0:T(8,128)}) %reduce-scatter.52.cloned.1.call-update) | async-done | bytes 524304 | tf_op jit(solution)/shard_map/reduce_scatter | solution.py:35
  196.6 41.2 %all-gather.46.cloned.1.call-done = bf16[1024,3,256]{0,2,1:T(8,128)(2,1)} async-done(((bf16[128,3,256]{0,2,1:T(8,128)(2,1)}), bf16[1024,3,256]{0,2,1:T(8,128)(2,1)}) %all-gather.46.cloned.1.call-update) | async-done | bytes 1572880 | tf_op jit(solution)/shard_map/all_gather | solution.py:23
  315.2 34.9 %all_gather.146 = bf16[1024,256]{1,0:T(8,128)(2,1)S(1)} all-gather(bf16[128,256]{1,0:T(8,128)(2,1)S(1)} %copy-done.113), channel_id=1, replica_groups=mesh['fsdp'=2,'ctx'=4,'tp'=4] {'fsdp','ctx'}, dimensions={0}, use_global_device_ids=true | all-gather | bytes 589824 | tf_op jit(solution)/shard_map/all_gather | solution.py:24
  356.6 24.6 %all-gather.94.cloned.1.call-done = bf16[2,1024,1,256]{1,3,2,0:T(8,128)(2,1)} async-done(((bf16[2,256,1,256]{1,3,2,0:T(8,128)(2,1)}), bf16[2,1024,1,256]{1,3,2,0:T(8,128)(2,1)}) %all-gather.94.cloned.1.call-update) | async-done | bytes 1048592 | tf_op jit(solution)/shard_map/all_gather | solution.py:79
  571.4 24.9 %reduce-scatter.42.cloned.1.call-done = f32[2,64,1024]{2,1,0:T(8,128)} async-done(((f32[2,256,1024]{2,1,0:T(8,128)}), f32[2,64,1024]{2,1,0:T(8,128)}) %reduce-scatter.42.cloned.1.call-update) | async-done | bytes 524304 | tf_op jit(solution)/shard_map/reduce_scatter | solution.py:35
  596.2 34.6 %reduce-scatter.48.cloned.1.call-done = f32[2,64,1024]{2,1,0:T(8,128)} async-done(((f32[2,256,1024]{2,1,0:T(8,128)}), f32[2,64,1024]{2,1,0:T(8,128)}) %reduce-scatter.48.cloned.1.call-update) | async-done | bytes 524304 | tf_op jit(solution)/shard_map/reduce_scatter | solution.py:35
  630.8 34.0 %reduce-scatter.54.cloned.1.call-done = f32[2,64,1024]{2,1,0:T(8,128)} async-done(((f32[2,256,1024]{2,1,0:T(8,128)}), f32[2,64,1024]{2,1,0:T(8,128)}) %reduce-scatter.54.cloned.1.call-update) | async-done | bytes 524304 | tf_op jit(solution)/shard_map/reduce_scatter | solution.py:35
  664.8 34.2 %reduce-scatter.36.cloned.1.call-done = f32[2,64,1024]{2,1,0:T(8,128)} async-done(((f32[2,256,1024]{2,1,0:T(8,128)}), f32[2,64,1024]{2,1,0:T(8,128)}) %reduce-scatter.36.cloned.1.call-update) | async-done | bytes 524304 | tf_op jit(solution)/shard_map/reduce_scatter | solution.py:35
  711.8 41.1 %all-gather.8 = f32[32,1,128]{2,1,0:T(1,128)S(1)} all-gather(f32[1,1,128]{2,1,0:T(1,128)S(1)} %bitcast.612), channel_id=1, replica_groups=mesh['fsdp'=2,'ctx'=4,'tp'=4] {'fsdp','ctx','tp'}, dimensions={0}, use_global_device_ids=true | all-gather | bytes 16896 | tf_op jit(solution)/shard_map/all_gather | solution.py:254
  855.1 38.8 %all-gather.52.cloned.1.call-done = bf16[1024,1024]{1,0:T(8,128)(2,1)} async-done(((bf16[128,1024]{1,0:T(8,128)(2,1)}), bf16[1024,1024]{1,0:T(8,128)(2,1)}) %all-gather.52.cloned.1.call-update) | async-done | bytes 2097168 | tf_op jit(solution)/shard_map/all_gather | solution.py:26
  956.7 24.9 %reduce-scatter.82.cloned.1.call-done = f32[2,64,1024]{2,1,0:T(8,128)} async-done(((f32[2,256,1024]{2,1,0:T(8,128)}), f32[2,64,1024]{2,1,0:T(8,128)}) %reduce-scatter.82.cloned.1.call-update) | async-done | bytes 524304 | tf_op jit(solution)/shard_map/reduce_scatter | solution.py:35
  983.5 32.9 %reduce-scatter.74.cloned.1.call-done = f32[2,64,1024]{2,1,0:T(8,128)} async-done(((f32[2,256,1024]{2,1,0:T(8,128)}), f32[2,64,1024]{2,1,0:T(8,128)}) %reduce-scatter.74.cloned.1.call-update) | async-done | bytes 524304 | tf_op jit(solution)/shard_map/reduce_scatter | solution.py:35
  1016.4 34.0 %reduce-scatter.66.cloned.1.call-done = f32[2,64,1024]{2,1,0:T(8,128)} async-done(((f32[2,256,1024]{2,1,0:T(8,128)}), f32[2,64,1024]{2,1,0:T(8,128)}) %reduce-scatter.66.cloned.1.call-update) | async-done | bytes 524304 | tf_op jit(solution)/shard_map/reduce_scatter | solution.py:35
  1050.3 34.0 %reduce-scatter.58.cloned.1.call-done = f32[2,64,1024]{2,1,0:T(8,128)} async-done(((f32[2,256,1024]{2,1,0:T(8,128)}), f32[2,64,1024]{2,1,0:T(8,128)}) %reduce-scatter.58.cloned.1.call-update) | async-done | bytes 524304 | tf_op jit(solution)/shard_map/reduce_scatter | solution.py:35
  1196.5 24.9 %reduce-scatter.84.cloned.1.call-done = bf16[2,256,256]{2,1,0:T(8,128)(2,1)} async-done(((bf16[2,1024,256]{2,1,0:T(8,128)(2,1)}), bf16[2,256,256]{2,1,0:T(8,128)(2,1)}) %reduce-scatter.84.cloned.1.call-update) | async-done | bytes 262160 | tf_op jit(solution)/shard_map/reduce_scatter | solution.py:172
  1249.3 28.2 %reduce-scatter.68.cloned.1.call-done = bf16[2,256,256]{2,1,0:T(8,128)(2,1)} async-done(((bf16[2,1024,256]{2,1,0:T(8,128)(2,1)}), bf16[2,256,256]{2,1,0:T(8,128)(2,1)}) %reduce-scatter.68.cloned.1.call-update) | async-done | bytes 262160 | tf_op jit(solution)/shard_map/reduce_scatter | solution.py:172
  1305.5 28.0 %reduce-scatter.60.cloned.1.call-done = bf16[2,256,256]{2,1,0:T(8,128)(2,1)} async-done(((bf16[2,1024,256]{2,1,0:T(8,128)(2,1)}), bf16[2,256,256]{2,1,0:T(8,128)(2,1)}) %reduce-scatter.60.cloned.1.call-update) | async-done | bytes 262160 | tf_op jit(solution)/shard_map/reduce_scatter | solution.py:172
  1361.5 28.1 %reduce-scatter.76.cloned.1.call-done = bf16[2,256,256]{2,1,0:T(8,128)(2,1)} async-done(((bf16[2,1024,256]{2,1,0:T(8,128)(2,1)}), bf16[2,256,256]{2,1,0:T(8,128)(2,1)}) %reduce-scatter.76.cloned.1.call-update) | async-done | bytes 262160 | tf_op jit(solution)/shard_map/reduce_scatter | solution.py:172
  1393.7 28.9 %reduce-scatter.88.cloned.1.call-done = f32[2,64,1024]{2,1,0:T(8,128)} async-done(((f32[2,256,1024]{2,1,0:T(8,128)}), f32[2,64,1024]{2,1,0:T(8,128)}) %reduce-scatter.88.cloned.1.call-update) | async-done | bytes 524304 | tf_op jit(solution)/shard_map/reduce_scatter | solution.py:35
  1422.7 34.7 %reduce-scatter.72.cloned.1.call-done = f32[2,64,1024]{2,1,0:T(8,128)} async-done(((f32[2,256,1024]{2,1,0:T(8,128)}), f32[2,64,1024]{2,1,0:T(8,128)}) %reduce-scatter.72.cloned.1.call-update) | async-done | bytes 524304 | tf_op jit(solution)/shard_map/reduce_scatter | solution.py:35
  1457.4 33.8 %reduce-scatter.64.cloned.1.call-done = f32[2,64,1024]{2,1,0:T(8,128)} async-done(((f32[2,256,1024]{2,1,0:T(8,128)}), f32[2,64,1024]{2,1,0:T(8,128)}) %reduce-scatter.64.cloned.1.call-update) | async-done | bytes 524304 | tf_op jit(solution)/shard_map/reduce_scatter | solution.py:35
  1491.2 34.2 %reduce-scatter.80.cloned.1.call-done = f32[2,64,1024]{2,1,0:T(8,128)} async-done(((f32[2,256,1024]{2,1,0:T(8,128)}), f32[2,64,1024]{2,1,0:T(8,128)}) %reduce-scatter.80.cloned.1.call-update) | async-done | bytes 524304 | tf_op jit(solution)/shard_map/reduce_scatter | solution.py:35
  1645.5 40.4 %all-reduce.15 = (f32[1024]{0:T(1024)S(1)}, f32[1024]{0:T(1024)S(1)}, f32[1024]{0:T(1024)S(1)}, f32[1024]{0:T(1024)S(1)}, f32[1024]{0:T(1024)S(1)}, /*index=5*/f...) all-reduce(f32[1024]{0:T(1024)S(1)} %dynamic-update-slice.9, ...), channel_id=1, replica_groups=mesh['fsdp'=2,'ctx'=4,'tp'=4] {'fsdp','ctx','tp'}, use_global_device_ids=true, to_apply=%add.6 | all-reduce | flops 12288 | bytes 98304
  1706.5 34.2 %reduce-scatter.56.cloned.1.call-done = f32[2,64,1024]{2,1,0:T(8,128)} async-done(((f32[2,256,1024]{2,1,0:T(8,128)}), f32[2,64,1024]{2,1,0:T(8,128)}) %reduce-scatter.56.cloned.1.call-update) | async-done | bytes 524304 | tf_op jit(solution)/shard_map/reduce_scatter | solution.py:35
  1752.1 59.7 %reduce-scatter.90.cloned.1.call-done = f32[128,2,256]{2,0,1:T(8,128)} async-done(((f32[1024,2,256]{2,0,1:T(8,128)}), f32[128,2,256]{2,0,1:T(8,128)}) %reduce-scatter.90.cloned.1.call-update) | async-done | bytes 262160 | tf_op jit(solution)/shard_map/reduce_scatter | solution.py:40
  1813.7 64.7 %reduce-scatter.94.cloned.1.call-done = f32[128,256]{1,0:T(8,128)} async-done(((f32[1024,256]{1,0:T(8,128)}), f32[128,256]{1,0:T(8,128)}) %reduce-scatter.94.cloned.1.call-update) | async-done | bytes 131088 | tf_op jit(solution)/shard_map/reduce_scatter | solution.py:42
  1878.3 91.6 %reduce-scatter.96.cloned.1.call-done = f32[128,1024]{1,0:T(8,128)} async-done(((f32[1024,1024]{1,0:T(8,128)}), f32[128,1024]{1,0:T(8,128)}) %reduce-scatter.96.cloned.1.call-update) | async-done | bytes 524304 | tf_op jit(solution)/shard_map/reduce_scatter | solution.py:43
  1969.9 91.7 %reduce-scatter.98.cloned.1.call-done = f32[128,1024]{1,0:T(8,128)} async-done(((f32[1024,1024]{1,0:T(8,128)}), f32[128,1024]{1,0:T(8,128)}) %reduce-scatter.98.cloned.1.call-update) | async-done | bytes 524304 | tf_op jit(solution)/shard_map/reduce_scatter | solution.py:44
  2061.6 79.3 %reduce-scatter.92.cloned.1.call-done = f32[128,3,256]{2,0,1:T(8,128)} async-done(((f32[1024,3,256]{2,0,1:T(8,128)}), f32[128,3,256]{2,0,1:T(8,128)}) %reduce-scatter.92.cloned.1.call-update) | async-done | bytes 393232 | tf_op jit(solution)/shard_map/reduce_scatter | solution.py:41
  (769 shorter events, 844.1 us)
Async XLA Ops:
  63.6 174.2 %all-gather.46.cloned.1.call-start = ((), (), s32[]{:S(2)}) async-start(), calls=%async_computation.36 | async-start | bytes 1769472 | tf_op jit(solution)/shard_map/all_gather | solution.py:23
  64.5 190.4 %all-gather.54.cloned.1.call-start = ((), (), s32[]{:S(2)}) async-start(), calls=%async_computation.43 | async-start | bytes 1310720 | tf_op jit(solution)/shard_map/all_gather | solution.py:31
  277.4 165.0 %all-gather.98.cloned.1.call-start = ((), (), s32[]{:S(2)}) async-start(), calls=%async_computation.94 | async-start | bytes 1310720 | tf_op jit(solution)/shard_map/all_gather | solution.py:79
  278.0 194.9 %all-gather.104.cloned.1.call-start = ((), (), s32[]{:S(2)}) async-start(), calls=%async_computation.97 | async-start | bytes 1310720 | tf_op jit(solution)/shard_map/all_gather | solution.py:78
  296.4 206.6 %all-gather.102.cloned.1.call-start = ((), (), s32[]{:S(2)}) async-start(), calls=%async_computation.96 | async-start | bytes 1310720 | tf_op jit(solution)/shard_map/all_gather | solution.py:79
  296.9 236.5 %all-gather.92.cloned.1.call-start = ((), (), s32[]{:S(2)}) async-start(), calls=%async_computation.91 | async-start | bytes 1310720 | tf_op jit(solution)/shard_map/all_gather | solution.py:78
  315.1 248.3 %all-gather.90.cloned.1.call-start = ((), (), s32[]{:S(2)}) async-start(), calls=%async_computation.90 | async-start | bytes 1310720 | tf_op jit(solution)/shard_map/all_gather | solution.py:79
  350.1 246.2 %reduce-scatter.42.cloned.1.call-start = ((), (), s32[]{:S(2)}) async-start(), calls=%async_computation.44 | async-start | bytes 2621440 | tf_op jit(solution)/shard_map/reduce_scatter | solution.py:35
  388.4 242.4 %reduce-scatter.48.cloned.1.call-start = ((), (), s32[]{:S(2)}) async-start(), calls=%async_computation.49 | async-start | bytes 2621440 | tf_op jit(solution)/shard_map/reduce_scatter | solution.py:35
  449.6 215.2 %reduce-scatter.54.cloned.1.call-start = ((), (), s32[]{:S(2)}) async-start(), calls=%async_computation.54 | async-start | bytes 2621440 | tf_op jit(solution)/shard_map/reduce_scatter | solution.py:35
  510.1 188.9 %reduce-scatter.36.cloned.1.call-start = ((), (), s32[]{:S(2)}) async-start(), calls=%async_computation.37 | async-start | bytes 2621440 | tf_op jit(solution)/shard_map/reduce_scatter | solution.py:35
  570.6 182.3 %all-gather.50.cloned.1.call-start = ((), (), s32[]{:S(2)}) async-start(), calls=%async_computation.39 | async-start | bytes 2359296 | tf_op jit(solution)/shard_map/all_gather | solution.py:25
  571.3 196.4 %all-gather.60.cloned.1.call-start = ((), (), s32[]{:S(2)}) async-start(), calls=%async_computation.50 | async-start | bytes 1310720 | tf_op jit(solution)/shard_map/all_gather | solution.py:31
  709.0 184.9 %all-gather.52.cloned.1.call-start = ((), (), s32[]{:S(2)}) async-start(), calls=%async_computation.40 | async-start | bytes 2359296 | tf_op jit(solution)/shard_map/all_gather | solution.py:26
  709.7 200.8 %all-gather.78.cloned.1.call-start = ((), (), s32[]{:S(2)}) async-start(), calls=%async_computation.71 | async-start | bytes 1310720 | tf_op jit(solution)/shard_map/all_gather | solution.py:31
  710.3 218.6 %all-gather.72.cloned.1.call-start = ((), (), s32[]{:S(2)}) async-start(), calls=%async_computation.64 | async-start | bytes 1310720 | tf_op jit(solution)/shard_map/all_gather | solution.py:31
  711.0 236.2 %all-gather.66.cloned.1.call-start = ((), (), s32[]{:S(2)}) async-start(), calls=%async_computation.57 | async-start | bytes 1310720 | tf_op jit(solution)/shard_map/all_gather | solution.py:31
  711.8 269.8 %reduce-scatter.82.cloned.1.call-start = ((), (), s32[]{:S(2)}) async-start(), calls=%async_computation.79 | async-start | bytes 2621440 | tf_op jit(solution)/shard_map/reduce_scatter | solution.py:35
  1158.4 175.1 %reduce-scatter.60.cloned.1.call-start = ((), (), s32[]{:S(2)}) async-start(), calls=%async_computation.60 | async-start | bytes 1310720 | tf_op jit(solution)/shard_map/reduce_scatter | solution.py:172
  1171.3 190.2 %reduce-scatter.78.cloned.1.call-start = ((), (), s32[]{:S(2)}) async-start(), calls=%async_computation.75 | async-start | bytes 1310720 | tf_op jit(solution)/shard_map/reduce_scatter | solution.py:178
  1179.7 209.9 %reduce-scatter.76.cloned.1.call-start = ((), (), s32[]{:S(2)}) async-start(), calls=%async_computation.74 | async-start | bytes 1310720 | tf_op jit(solution)/shard_map/reduce_scatter | solution.py:172
  1192.6 230.0 %reduce-scatter.88.cloned.1.call-start = ((), (), s32[]{:S(2)}) async-start(), calls=%async_computation.83 | async-start | bytes 2621440 | tf_op jit(solution)/shard_map/reduce_scatter | solution.py:35
  1225.2 232.2 %reduce-scatter.72.cloned.1.call-start = ((), (), s32[]{:S(2)}) async-start(), calls=%async_computation.69 | async-start | bytes 2621440 | tf_op jit(solution)/shard_map/reduce_scatter | solution.py:35
  1281.4 209.8 %reduce-scatter.64.cloned.1.call-start = ((), (), s32[]{:S(2)}) async-start(), calls=%async_computation.62 | async-start | bytes 2621440 | tf_op jit(solution)/shard_map/reduce_scatter | solution.py:35
  1337.5 187.9 %reduce-scatter.80.cloned.1.call-start = ((), (), s32[]{:S(2)}) async-start(), calls=%async_computation.76 | async-start | bytes 2621440 | tf_op jit(solution)/shard_map/reduce_scatter | solution.py:35
  1544.3 162.2 %reduce-scatter.50.cloned.1.call-start = ((), (), s32[]{:S(2)}) async-start(), calls=%async_computation.51 | async-start | bytes 2621440 | tf_op jit(solution)/shard_map/reduce_scatter | solution.py:35
  1548.1 192.5 %reduce-scatter.56.cloned.1.call-start = ((), (), s32[]{:S(2)}) async-start(), calls=%async_computation.56 | async-start | bytes 2621440 | tf_op jit(solution)/shard_map/reduce_scatter | solution.py:35
  1552.0 259.8 %reduce-scatter.90.cloned.1.call-start = ((), (), s32[]{:S(2)}) async-start(), calls=%async_computation.85 | async-start | bytes 2359296 | tf_op jit(solution)/shard_map/reduce_scatter | solution.py:40
  1608.8 269.6 %reduce-scatter.94.cloned.1.call-start = ((), (), s32[]{:S(2)}) async-start(), calls=%async_computation.87 | async-start | bytes 1179648 | tf_op jit(solution)/shard_map/reduce_scatter | solution.py:42
  1615.1 354.7 %reduce-scatter.96.cloned.1.call-start = ((), (), s32[]{:S(2)}) async-start(), calls=%async_computation.88 | async-start | bytes 4718592 | tf_op jit(solution)/shard_map/reduce_scatter | solution.py:43
  1624.7 436.9 %reduce-scatter.98.cloned.1.call-start = ((), (), s32[]{:S(2)}) async-start(), calls=%async_computation.89 | async-start | bytes 4718592 | tf_op jit(solution)/shard_map/reduce_scatter | solution.py:44
  1635.1 505.9 %reduce-scatter.92.cloned.1.call-start = ((), (), s32[]{:S(2)}) async-start(), calls=%async_computation.86 | async-start | bytes 3538944 | tf_op jit(solution)/shard_map/reduce_scatter | solution.py:41
  (226 other events, 11546.0 us)
Sparse Core Ops, SparseCore 0:
  10.7 42.8 all-gather.41
  57.1 30.3 reduce-scatter.33
  90.8 31.4 reduce-scatter.39
  124.7 31.3 reduce-scatter.45
  158.6 31.4 reduce-scatter.51
  192.5 45.3 all-gather.45
  313.6 37.0 all-gather.95
  352.7 28.5 all-gather.93
  504.9 28.4 all-gather.91
  566.5 29.7 reduce-scatter.41
  599.3 31.4 reduce-scatter.47
  633.4 31.3 reduce-scatter.53
  667.5 31.4 reduce-scatter.35
  701.1 49.2 all-gather.49
  844.6 49.2 all-gather.51
  950.2 31.4 reduce-scatter.81
  984.9 31.4 reduce-scatter.73
  1018.9 31.4 reduce-scatter.65
  1052.9 31.4 reduce-scatter.57
  1392.6 30.0 reduce-scatter.87
  1425.9 31.4 reduce-scatter.71
  1459.8 31.4 reduce-scatter.63
  1493.9 31.4 reduce-scatter.79
  1606.5 31.4 reduce-scatter.37
  1641.1 31.5 reduce-scatter.43
  1675.1 31.3 reduce-scatter.49
  1709.2 31.4 reduce-scatter.55
  1744.2 67.5 reduce-scatter.89
  1815.8 62.4 reduce-scatter.93
  1882.8 87.0 reduce-scatter.95
  1973.9 87.6 reduce-scatter.97
  2066.2 74.6 reduce-scatter.91
  (33 shorter events, 677.9 us)
where the time goes:
time: 2160 us; the launch traced here: 2150 us
  waiting for transfers between devices  1570 us (73%)
  matrix products  256 us (12%)
  blocking collectives  155 us (7%)
  other arithmetic  86.4 us (4%)
  local copies, waits for them, and re-layouts  58.5 us (3%)
    reduce_scatter x20, waiting for transfers between devices, fold_rows(): return lax.psum_scatter(block, 'tp', scatter_dimension=1, tiled=True)  519 us
    all_gather x20, waiting for transfers between devices, spread_rows(): return lax.all_gather(block, 'tp', axis=1, tiled=True)  196 us
    reduce_scatter x4, waiting for transfers between devices, micro_step(): lax.psum_scatter(key_terms.reshape(groups, seq_len, heads_dev * HD).astyp...  109 us
    all_gather x4, waiting for transfers between devices, micro_step(): lax.all_gather(project[:, :, 2], 'ctx', axis=1, tiled=True)  97.3 us
    reduce_scatter x1, waiting for transfers between devices, reduce_weights(): lax.psum_scatter(parts[4], ('fsdp', 'ctx'), scatter_dimension=0, tiled=True)  91.7 us
    reduce_scatter x1, waiting for transfers between devices, reduce_weights(): lax.psum_scatter(parts[3], ('fsdp', 'ctx'), scatter_dimension=0, tiled=True)  91.6 us
    reduce_scatter x1, waiting for transfers between devices, reduce_weights(): lax.psum_scatter(parts[1], ('fsdp', 'ctx'), scatter_dimension=0, tiled=True)  79.3 us
    unnamed x2, blocking collectives  79.3 us
  transfers between devices with their start and end apart: 65, of which 55 were waited for; matrix products, arithmetic and copies ran while one was open for 16% of the time, Pallas kernels for 0%

commit v1 on v0

--- a/solution.py
+++ b/solution.py
@@ -5,6 +5,23 @@
 
 HD = 64
 EPSILON = 1e-05
+
+
+def attach_point(body, a_name):
+    piece_next = lax.axis_size(a_name)
+    small = lax.axis_index(a_name)
+    u_next, plain = (piece_next, small)
+    row_out, high = (body, 1)
+    while high < u_next:
+        parts_seen = []
+        for k in range(u_next):
+            parts_seen.append((k, k ^ high))
+        view_out = lax.ppermute(row_out, axis_name=a_name, perm=parts_seen)
+        arr_next = jnp.concatenate([row_out, view_out], axis=1)
+        shaped = jnp.concatenate([view_out, row_out], axis=1)
+        row_out = jnp.where(plain & high == 0, arr_next, shaped)
+        high = 2 * high
+    return row_out
 
 
 def layer_norm(matrix, scales, shifts):
@@ -75,7 +92,7 @@
         "std,dcj->stcj", normed_all, attend_full, preferred_element_type=jnp.float32
     ).astype(jnp.bfloat16)
     key_rows, value_rows = (
-        lax.all_gather(project[:, :, 1], "ctx", axis=1, tiled=True),
+        attach_point(project[:, :, 1], "ctx"),
         lax.all_gather(project[:, :, 2], "ctx", axis=1, tiled=True),
     )
     seq_len = key_rows.shape[1]

time: 2160 us -> 2080 us (0.963)
  waiting for transfers between devices: 1570 us -> 1480 us
    ppermute x0 -> x8, waiting for transfers between devices: none -> 153 us  [attach_point(): view_out = lax.ppermute(row_out, axis_name=a_name, perm=parts_seen)]
    all_gather x4, waiting for transfers between devices: 97.3 us -> 0.01 us  [micro_step(): lax.all_gather(project[:, :, 2], 'ctx', axis=1, tiled=True)]
    all_gather x4 -> x0, waiting for transfers between devices: 70.1 us -> none  [micro_step(): lax.all_gather(project[:, :, 1], 'ctx', axis=1, tiled=True)]
    reduce_scatter x20, waiting for transfers between devices: 519 us -> 459 us  [fold_rows(): return lax.psum_scatter(block, 'tp', scatter_dimension=1, tiled=True)]
  transfers between devices with their start and end apart: 65 -> 69, of which waited for: 55 -> 51; matrix products, arithmetic and copies ran while one was open for 16% -> 17% of each run, Pallas kernels for 0% -> 0%
where the time goes in v1:
time: 2080 us; the launch traced here: 2070 us
  waiting for transfers between devices  1480 us (71%)
  matrix products  252 us (12%)
  blocking collectives  158 us (8%)
  other arithmetic  90.2 us (4%)
  local copies, waits for them, and re-layouts  58.3 us (3%)
    reduce_scatter x20, waiting for transfers between devices, fold_rows(): return lax.psum_scatter(block, 'tp', scatter_dimension=1, tiled=True)  459 us
    all_gather x20, waiting for transfers between devices, spread_rows(): return lax.all_gather(block, 'tp', axis=1, tiled=True)  183 us
    ppermute x8, waiting for transfers between devices, attach_point(): view_out = lax.ppermute(row_out, axis_name=a_name, perm=parts_seen)  153 us
    reduce_scatter x4, waiting for transfers between devices, micro_step(): lax.psum_scatter(key_terms.reshape(groups, seq_len, heads_dev * HD).astyp...  109 us
    reduce_scatter x1, waiting for transfers between devices, reduce_weights(): lax.psum_scatter(parts[4], ('fsdp', 'ctx'), scatter_dimension=0, tiled=True)  91.9 us
    reduce_scatter x1, waiting for transfers between devices, reduce_weights(): lax.psum_scatter(parts[3], ('fsdp', 'ctx'), scatter_dimension=0, tiled=True)  91.4 us
    reduce_scatter x1, waiting for transfers between devices, reduce_weights(): lax.psum_scatter(parts[1], ('fsdp', 'ctx'), scatter_dimension=0, tiled=True)  79.4 us
    unnamed x2, blocking collectives  79.2 us
  transfers between devices with their start and end apart: 69, of which 51 were waited for; matrix products, arithmetic and copies ran while one was open for 17% of the time, Pallas kernels for 0%

profile of v1, /device:TPU:0, one launch (start us, length us, event | category | flops | bytes accessed | tf_op | source)
XLA Modules:
  0.0 2067.9 jit_solution(2710852898366245291)
XLA Ops:
  10.6 43.0 %all-gather.34.cloned.1.call-done = bf16[1024,2,256]{2,0,1:T(8,128)(2,1)} async-done(((bf16[128,2,256]{2,0,1:T(8,128)(2,1)}), bf16[1024,2,256]{2,0,1:T(8,128)(2,1)}) %all-gather.34.cloned.1.call-update) | async-done | bytes 1048592 | tf_op jit(solution)/shard_map/all_gather | solution.py:39
  65.9 38.9 %all-reduce.16 = (f32[1024]{0:T(1024)S(1)}, f32[1024]{0:T(1024)S(1)}, f32[1024]{0:T(1024)S(1)}, f32[1024]{0:T(1024)S(1)}, f32[1024]{0:T(1024)S(1)}, /*index=5*/f32[1024]{0:T(1024)S(1)}) all-reduce(f32[1024]{0:T(1024)S(1)} %dynamic-update-slice.3, ...), channel_id=1, replica_groups=mesh['fsdp'=2,'ctx'=4,'tp'=4] {'fsdp','ctx','tp'}, use_global_device_ids=true, to_apply=%add | all-reduce | flops 6144 | bytes 49152
  122.3 33.8 %reduce-scatter.46.cloned.1.call-done = f32[2,64,1024]{2,1,0:T(8,128)} async-done(((f32[2,256,1024]{2,1,0:T(8,128)}), f32[2,64,1024]{2,1,0:T(8,128)}) %reduce-scatter.46.cloned.1.call-update) | async-done | bytes 524304 | tf_op jit(solution)/shard_map/reduce_scatter | solution.py:52
  156.1 34.0 %reduce-scatter.52.cloned.1.call-done = f32[2,64,1024]{2,1,0:T(8,128)} async-done(((f32[2,256,1024]{2,1,0:T(8,128)}), f32[2,64,1024]{2,1,0:T(8,128)}) %reduce-scatter.52.cloned.1.call-update) | async-done | bytes 524304 | tf_op jit(solution)/shard_map/reduce_scatter | solution.py:52
  196.7 41.3 %all-gather.38.cloned.1.call-done = bf16[1024,3,256]{0,2,1:T(8,128)(2,1)} async-done(((bf16[128,3,256]{0,2,1:T(8,128)(2,1)}), bf16[1024,3,256]{0,2,1:T(8,128)(2,1)}) %all-gather.38.cloned.1.call-update) | async-done | bytes 1572880 | tf_op jit(solution)/shard_map/all_gather | solution.py:40
  298.0 37.6 %all_gather.133 = bf16[1024,256]{1,0:T(8,128)(2,1)S(1)} all-gather(bf16[128,256]{1,0:T(8,128)(2,1)S(1)} %copy-done.126), channel_id=1, replica_groups=mesh['fsdp'=2,'ctx'=4,'tp'=4] {'fsdp','ctx'}, dimensions={0}, use_global_device_ids=true | all-gather | bytes 589824 | tf_op jit(solution)/shard_map/all_gather | solution.py:41
  341.6 24.8 %collective-permute-done.3 = bf16[2,512,256]{1,2,0:T(8,128)(2,1)} collective-permute-done((bf16[2,512,256]{1,2,0:T(8,128)(2,1)}, bf16[2,512,256]{1,2,0:T(8,128)(2,1)}, u32[]{:S(2)}, u32[]{:S(2)}) %collective-permute-start.3) | collective-permute-done | bytes 524320 | tf_op jit(solution)/shard_map/ppermute | solution.py:19
  396.1 40.1 %collective-permute-done.5 = bf16[2,512,256]{1,2,0:T(8,128)(2,1)S(1)} collective-permute-done((bf16[2,512,256]{1,2,0:T(8,128)(2,1)S(1)}, bf16[2,512,256]{1,2,0:T(8,128)(2,1)S(1)}, u32[]{:S(2)}, u32[]{:S(2)}) %collective-permute-start.5) | collective-permute-done | bytes 524320 | tf_op jit(solution)/shard_map/ppermute | solution.py:19
  466.8 26.3 %collective-permute-done.7 = bf16[2,512,256]{1,2,0:T(8,128)(2,1)S(1)} collective-permute-done((bf16[2,512,256]{1,2,0:T(8,128)(2,1)S(1)}, bf16[2,512,256]{1,2,0:T(8,128)(2,1)S(1)}, u32[]{:S(2)}, u32[]{:S(2)}) %collective-permute-start.7) | collective-permute-done | bytes 524320 | tf_op jit(solution)/shard_map/ppermute | solution.py:19
  513.6 24.9 %collective-permute-done.1 = bf16[2,512,256]{1,2,0:T(8,128)(2,1)S(1)} collective-permute-done((bf16[2,512,256]{1,2,0:T(8,128)(2,1)S(1)}, bf16[2,512,256]{1,2,0:T(8,128)(2,1)S(1)}, u32[]{:S(2)}, u32[]{:S(2)}) %collective-permute-start.1) | collective-permute-done | bytes 524320 | tf_op jit(solution)/shard_map/ppermute | solution.py:19
  551.3 33.1 %reduce-scatter.54.cloned.1.call-done = f32[2,64,1024]{2,1,0:T(8,128)} async-done(((f32[2,256,1024]{2,1,0:T(8,128)}), f32[2,64,1024]{2,1,0:T(8,128)}) %reduce-scatter.54.cloned.1.call-update) | async-done | bytes 524304 | tf_op jit(solution)/shard_map/reduce_scatter | solution.py:52
  584.4 34.0 %reduce-scatter.36.cloned.1.call-done = f32[2,64,1024]{2,1,0:T(8,128)} async-done(((f32[2,256,1024]{2,1,0:T(8,128)}), f32[2,64,1024]{2,1,0:T(8,128)}) %reduce-scatter.36.cloned.1.call-update) | async-done | bytes 524304 | tf_op jit(solution)/shard_map/reduce_scatter | solution.py:52
  631.4 41.2 %all-gather.4 = f32[32,1,128]{2,1,0:T(1,128)S(1)} all-gather(f32[1,1,128]{2,1,0:T(1,128)S(1)} %bitcast.622), channel_id=1, replica_groups=mesh['fsdp'=2,'ctx'=4,'tp'=4] {'fsdp','ctx','tp'}, dimensions={0}, use_global_device_ids=true | all-gather | bytes 16896 | tf_op jit(solution)/shard_map/all_gather | solution.py:271
  774.9 38.8 %all-gather.44.cloned.1.call-done = bf16[1024,1024]{1,0:T(8,128)(2,1)} async-done(((bf16[128,1024]{1,0:T(8,128)(2,1)}), bf16[1024,1024]{1,0:T(8,128)(2,1)}) %all-gather.44.cloned.1.call-update) | async-done | bytes 2097168 | tf_op jit(solution)/shard_map/all_gather | solution.py:43
  876.3 25.1 %reduce-scatter.82.cloned.1.call-done = f32[2,64,1024]{2,1,0:T(8,128)} async-done(((f32[2,256,1024]{2,1,0:T(8,128)}), f32[2,64,1024]{2,1,0:T(8,128)}) %reduce-scatter.82.cloned.1.call-update) | async-done | bytes 524304 | tf_op jit(solution)/shard_map/reduce_scatter | solution.py:52
  903.2 32.7 %reduce-scatter.74.cloned.1.call-done = f32[2,64,1024]{2,1,0:T(8,128)} async-done(((f32[2,256,1024]{2,1,0:T(8,128)}), f32[2,64,1024]{2,1,0:T(8,128)}) %reduce-scatter.74.cloned.1.call-update) | async-done | bytes 524304 | tf_op jit(solution)/shard_map/reduce_scatter | solution.py:52
  935.9 34.0 %reduce-scatter.66.cloned.1.call-done = f32[2,64,1024]{2,1,0:T(8,128)} async-done(((f32[2,256,1024]{2,1,0:T(8,128)}), f32[2,64,1024]{2,1,0:T(8,128)}) %reduce-scatter.66.cloned.1.call-update) | async-done | bytes 524304 | tf_op jit(solution)/shard_map/reduce_scatter | solution.py:52
  969.9 34.1 %reduce-scatter.58.cloned.1.call-done = f32[2,64,1024]{2,1,0:T(8,128)} async-done(((f32[2,256,1024]{2,1,0:T(8,128)}), f32[2,64,1024]{2,1,0:T(8,128)}) %reduce-scatter.58.cloned.1.call-update) | async-done | bytes 524304 | tf_op jit(solution)/shard_map/reduce_scatter | solution.py:52
  1168.9 28.2 %reduce-scatter.68.cloned.1.call-done = bf16[2,256,256]{2,1,0:T(8,128)(2,1)} async-done(((bf16[2,1024,256]{2,1,0:T(8,128)(2,1)}), bf16[2,256,256]{2,1,0:T(8,128)(2,1)}) %reduce-scatter.68.cloned.1.call-update) | async-done | bytes 262160 | tf_op jit(solution)/shard_map/reduce_scatter | solution.py:189
  1225.3 28.2 %reduce-scatter.60.cloned.1.call-done = bf16[2,256,256]{2,1,0:T(8,128)(2,1)} async-done(((bf16[2,1024,256]{2,1,0:T(8,128)(2,1)}), bf16[2,256,256]{2,1,0:T(8,128)(2,1)}) %reduce-scatter.60.cloned.1.call-update) | async-done | bytes 262160 | tf_op jit(solution)/shard_map/reduce_scatter | solution.py:189
  1281.5 28.2 %reduce-scatter.76.cloned.1.call-done = bf16[2,256,256]{2,1,0:T(8,128)(2,1)} async-done(((bf16[2,1024,256]{2,1,0:T(8,128)(2,1)}), bf16[2,256,256]{2,1,0:T(8,128)(2,1)}) %reduce-scatter.76.cloned.1.call-update) | async-done | bytes 262160 | tf_op jit(solution)/shard_map/reduce_scatter | solution.py:189
  1313.8 29.0 %reduce-scatter.88.cloned.1.call-done = f32[2,64,1024]{2,1,0:T(8,128)} async-done(((f32[2,256,1024]{2,1,0:T(8,128)}), f32[2,64,1024]{2,1,0:T(8,128)}) %reduce-scatter.88.cloned.1.call-update) | async-done | bytes 524304 | tf_op jit(solution)/shard_map/reduce_scatter | solution.py:52
  1342.7 34.5 %reduce-scatter.72.cloned.1.call-done = f32[2,64,1024]{2,1,0:T(8,128)} async-done(((f32[2,256,1024]{2,1,0:T(8,128)}), f32[2,64,1024]{2,1,0:T(8,128)}) %reduce-scatter.72.cloned.1.call-update) | async-done | bytes 524304 | tf_op jit(solution)/shard_map/reduce_scatter | solution.py:52
  1377.3 33.9 %reduce-scatter.64.cloned.1.call-done = f32[2,64,1024]{2,1,0:T(8,128)} async-done(((f32[2,256,1024]{2,1,0:T(8,128)}), f32[2,64,1024]{2,1,0:T(8,128)}) %reduce-scatter.64.cloned.1.call-update) | async-done | bytes 524304 | tf_op jit(solution)/shard_map/reduce_scatter | solution.py:52
  1411.1 34.0 %reduce-scatter.80.cloned.1.call-done = f32[2,64,1024]{2,1,0:T(8,128)} async-done(((f32[2,256,1024]{2,1,0:T(8,128)}), f32[2,64,1024]{2,1,0:T(8,128)}) %reduce-scatter.80.cloned.1.call-update) | async-done | bytes 524304 | tf_op jit(solution)/shard_map/reduce_scatter | solution.py:52
  1565.1 40.3 %all-reduce.15 = (f32[1024]{0:T(1024)S(1)}, f32[1024]{0:T(1024)S(1)}, f32[1024]{0:T(1024)S(1)}, f32[1024]{0:T(1024)S(1)}, f32[1024]{0:T(1024)S(1)}, /*index=5*/f...) all-reduce(f32[1024]{0:T(1024)S(1)} %dynamic-update-slice.9, ...), channel_id=1, replica_groups=mesh['fsdp'=2,'ctx'=4,'tp'=4] {'fsdp','ctx','tp'}, use_global_device_ids=true, to_apply=%add.6 | all-reduce | flops 12288 | bytes 98304
  1626.2 34.2 %reduce-scatter.56.cloned.1.call-done = f32[2,64,1024]{2,1,0:T(8,128)} async-done(((f32[2,256,1024]{2,1,0:T(8,128)}), f32[2,64,1024]{2,1,0:T(8,128)}) %reduce-scatter.56.cloned.1.call-update) | async-done | bytes 524304 | tf_op jit(solution)/shard_map/reduce_scatter | solution.py:52
  1671.8 60.0 %reduce-scatter.90.cloned.1.call-done = f32[128,2,256]{2,0,1:T(8,128)} async-done(((f32[1024,2,256]{2,0,1:T(8,128)}), f32[128,2,256]{2,0,1:T(8,128)}) %reduce-scatter.90.cloned.1.call-update) | async-done | bytes 262160 | tf_op jit(solution)/shard_map/reduce_scatter | solution.py:57
  1733.6 64.5 %reduce-scatter.94.cloned.1.call-done = f32[128,256]{1,0:T(8,128)} async-done(((f32[1024,256]{1,0:T(8,128)}), f32[128,256]{1,0:T(8,128)}) %reduce-scatter.94.cloned.1.call-update) | async-done | bytes 131088 | tf_op jit(solution)/shard_map/reduce_scatter | solution.py:59
  1798.1 91.4 %reduce-scatter.96.cloned.1.call-done = f32[128,1024]{1,0:T(8,128)} async-done(((f32[1024,1024]{1,0:T(8,128)}), f32[128,1024]{1,0:T(8,128)}) %reduce-scatter.96.cloned.1.call-update) | async-done | bytes 524304 | tf_op jit(solution)/shard_map/reduce_scatter | solution.py:60
  1889.5 91.9 %reduce-scatter.98.cloned.1.call-done = f32[128,1024]{1,0:T(8,128)} async-done(((f32[1024,1024]{1,0:T(8,128)}), f32[128,1024]{1,0:T(8,128)}) %reduce-scatter.98.cloned.1.call-update) | async-done | bytes 524304 | tf_op jit(solution)/shard_map/reduce_scatter | solution.py:61
  1981.4 79.4 %reduce-scatter.92.cloned.1.call-done = f32[128,3,256]{2,0,1:T(8,128)} async-done(((f32[1024,3,256]{2,0,1:T(8,128)}), f32[128,3,256]{2,0,1:T(8,128)}) %reduce-scatter.92.cloned.1.call-update) | async-done | bytes 393232 | tf_op jit(solution)/shard_map/reduce_scatter | solution.py:58
  (809 shorter events, 754.6 us)
Async XLA Ops:
  63.6 174.3 %all-gather.38.cloned.1.call-start = ((), (), s32[]{:S(2)}) async-start(), calls=%async_computation.36 | async-start | bytes 1769472 | tf_op jit(solution)/shard_map/all_gather | solution.py:40
  64.5 190.5 %all-gather.46.cloned.1.call-start = ((), (), s32[]{:S(2)}) async-start(), calls=%async_computation.43 | async-start | bytes 1310720 | tf_op jit(solution)/shard_map/all_gather | solution.py:48
  196.6 175.8 %all-gather.84.cloned.1.call-start = ((), (), s32[]{:S(2)}) async-start(), calls=%async_computation.91 | async-start | bytes 1310720 | tf_op jit(solution)/shard_map/all_gather | solution.py:96
  258.6 182.3 %all-gather.86.cloned.1.call-start = ((), (), s32[]{:S(2)}) async-start(), calls=%async_computation.92 | async-start | bytes 1310720 | tf_op jit(solution)/shard_map/all_gather | solution.py:96
  277.6 220.3 %all-gather.88.cloned.1.call-start = ((), (), s32[]{:S(2)}) async-start(), calls=%async_computation.93 | async-start | bytes 1310720 | tf_op jit(solution)/shard_map/all_gather | solution.py:96
  296.4 246.8 %all-gather.82.cloned.1.call-start = ((), (), s32[]{:S(2)}) async-start(), calls=%async_computation.90 | async-start | bytes 1310720 | tf_op jit(solution)/shard_map/all_gather | solution.py:96
  340.2 211.1 %reduce-scatter.42.cloned.1.call-start = ((), (), s32[]{:S(2)}) async-start(), calls=%async_computation.44 | async-start | bytes 2621440 | tf_op jit(solution)/shard_map/reduce_scatter | solution.py:52
  379.6 171.7 %reduce-scatter.48.cloned.1.call-start = ((), (), s32[]{:S(2)}) async-start(), calls=%async_computation.49 | async-start | bytes 2621440 | tf_op jit(solution)/shard_map/reduce_scatter | solution.py:52
  628.7 185.0 %all-gather.44.cloned.1.call-start = ((), (), s32[]{:S(2)}) async-start(), calls=%async_computation.40 | async-start | bytes 2359296 | tf_op jit(solution)/shard_map/all_gather | solution.py:43
  629.4 200.9 %all-gather.70.cloned.1.call-start = ((), (), s32[]{:S(2)}) async-start(), calls=%async_computation.71 | async-start | bytes 1310720 | tf_op jit(solution)/shard_map/all_gather | solution.py:48
  630.0 218.5 %all-gather.64.cloned.1.call-start = ((), (), s32[]{:S(2)}) async-start(), calls=%async_computation.64 | async-start | bytes 1310720 | tf_op jit(solution)/shard_map/all_gather | solution.py:48
  630.6 236.2 %all-gather.58.cloned.1.call-start = ((), (), s32[]{:S(2)}) async-start(), calls=%async_computation.57 | async-start | bytes 1310720 | tf_op jit(solution)/shard_map/all_gather | solution.py:48
  631.3 270.0 %reduce-scatter.82.cloned.1.call-start = ((), (), s32[]{:S(2)}) async-start(), calls=%async_computation.79 | async-start | bytes 2621440 | tf_op jit(solution)/shard_map/reduce_scatter | solution.py:52
  876.3 150.6 %all-gather.78.cloned.1.call-start = ((), (), s32[]{:S(2)}) async-start(), calls=%async_computation.80 | async-start | bytes 1310720 | tf_op jit(solution)/shard_map/all_gather | solution.py:48
  1069.8 155.4 %reduce-scatter.62.cloned.1.call-start = ((), (), s32[]{:S(2)}) async-start(), calls=%async_computation.61 | async-start | bytes 1310720 | tf_op jit(solution)/shard_map/reduce_scatter | solution.py:195
  1078.2 175.3 %reduce-scatter.60.cloned.1.call-start = ((), (), s32[]{:S(2)}) async-start(), calls=%async_computation.60 | async-start | bytes 1310720 | tf_op jit(solution)/shard_map/reduce_scatter | solution.py:189
  1091.1 190.4 %reduce-scatter.78.cloned.1.call-start = ((), (), s32[]{:S(2)}) async-start(), calls=%async_computation.75 | async-start | bytes 1310720 | tf_op jit(solution)/shard_map/reduce_scatter | solution.py:195
  1099.4 210.3 %reduce-scatter.76.cloned.1.call-start = ((), (), s32[]{:S(2)}) async-start(), calls=%async_computation.74 | async-start | bytes 1310720 | tf_op jit(solution)/shard_map/reduce_scatter | solution.py:189
  1112.4 230.3 %reduce-scatter.88.cloned.1.call-start = ((), (), s32[]{:S(2)}) async-start(), calls=%async_computation.83 | async-start | bytes 2621440 | tf_op jit(solution)/shard_map/reduce_scatter | solution.py:52
  1144.8 232.4 %reduce-scatter.72.cloned.1.call-start = ((), (), s32[]{:S(2)}) async-start(), calls=%async_computation.69 | async-start | bytes 2621440 | tf_op jit(solution)/shard_map/reduce_scatter | solution.py:52
  1200.5 210.6 %reduce-scatter.64.cloned.1.call-start = ((), (), s32[]{:S(2)}) async-start(), calls=%async_computation.62 | async-start | bytes 2621440 | tf_op jit(solution)/shard_map/reduce_scatter | solution.py:52
  1257.4 187.7 %reduce-scatter.80.cloned.1.call-start = ((), (), s32[]{:S(2)}) async-start(), calls=%async_computation.76 | async-start | bytes 2621440 | tf_op jit(solution)/shard_map/reduce_scatter | solution.py:52
  1313.7 158.0 %all-gather.74.cloned.1.call-start = ((), (), s32[]{:S(2)}) async-start(), calls=%async_computation.77 | async-start | bytes 1310720 | tf_op jit(solution)/shard_map/all_gather | solution.py:48
  1455.6 154.5 %reduce-scatter.38.cloned.1.call-start = ((), (), s32[]{:S(2)}) async-start(), calls=%async_computation.41 | async-start | bytes 2621440 | tf_op jit(solution)/shard_map/reduce_scatter | solution.py:52
  1460.2 149.9 %reduce-scatter.44.cloned.1.call-start = ((), (), s32[]{:S(2)}) async-start(), calls=%async_computation.46 | async-start | bytes 2621440 | tf_op jit(solution)/shard_map/reduce_scatter | solution.py:52
  1464.0 162.2 %reduce-scatter.50.cloned.1.call-start = ((), (), s32[]{:S(2)}) async-start(), calls=%async_computation.51 | async-start | bytes 2621440 | tf_op jit(solution)/shard_map/reduce_scatter | solution.py:52
  1467.8 192.5 %reduce-scatter.56.cloned.1.call-start = ((), (), s32[]{:S(2)}) async-start(), calls=%async_computation.56 | async-start | bytes 2621440 | tf_op jit(solution)/shard_map/reduce_scatter | solution.py:52
  1471.7 260.1 %reduce-scatter.90.cloned.1.call-start = ((), (), s32[]{:S(2)}) async-start(), calls=%async_computation.85 | async-start | bytes 2359296 | tf_op jit(solution)/shard_map/reduce_scatter | solution.py:57
  1528.3 269.8 %reduce-scatter.94.cloned.1.call-start = ((), (), s32[]{:S(2)}) async-start(), calls=%async_computation.87 | async-start | bytes 1179648 | tf_op jit(solution)/shard_map/reduce_scatter | solution.py:59
  1534.7 354.8 %reduce-scatter.96.cloned.1.call-start = ((), (), s32[]{:S(2)}) async-start(), calls=%async_computation.88 | async-start | bytes 4718592 | tf_op jit(solution)/shard_map/reduce_scatter | solution.py:60
  1544.2 437.2 %reduce-scatter.98.cloned.1.call-start = ((), (), s32[]{:S(2)}) async-start(), calls=%async_computation.89 | async-start | bytes 4718592 | tf_op jit(solution)/shard_map/reduce_scatter | solution.py:61
  1554.7 506.2 %reduce-scatter.92.cloned.1.call-start = ((), (), s32[]{:S(2)}) async-start(), calls=%async_computation.86 | async-start | bytes 3538944 | tf_op jit(solution)/shard_map/reduce_scatter | solution.py:58
  (244 other events, 11291.8 us)
Sparse Core Ops, SparseCore 0:
  10.7 42.8 all-gather.33
  57.1 30.3 reduce-scatter.33
  90.8 31.4 reduce-scatter.39
  124.7 31.3 reduce-scatter.45
  158.6 31.4 reduce-scatter.51
  192.6 45.3 all-gather.37
  313.7 47.3 all-gather.83
  362.5 33.3 all-gather.85
  397.5 37.4 all-gather.87
  436.3 48.4 all-gather.81
  519.1 31.4 reduce-scatter.47
  553.0 31.4 reduce-scatter.53
  587.0 31.3 reduce-scatter.35
  620.5 49.4 all-gather.41
  764.3 49.2 all-gather.43
  869.9 31.4 reduce-scatter.81
  904.5 31.3 reduce-scatter.73
  938.5 31.4 reduce-scatter.65
  972.6 31.3 reduce-scatter.57
  1312.6 30.0 reduce-scatter.87
  1345.8 31.3 reduce-scatter.71
  1379.6 31.4 reduce-scatter.63
  1413.7 31.3 reduce-scatter.79
  1526.0 31.4 reduce-scatter.37
  1560.7 31.5 reduce-scatter.43
  1594.8 31.3 reduce-scatter.49
  1628.9 31.4 reduce-scatter.55
  1663.9 67.8 reduce-scatter.89
  1735.6 62.4 reduce-scatter.93
  1802.6 86.8 reduce-scatter.95
  1893.8 87.6 reduce-scatter.97
  1986.1 74.7 reduce-scatter.91
  (29 shorter events, 563.9 us)
